TPU v7x, 32 devices: a whole 2x2x4 slice. The times are simulated.
32 devices in a mesh: rep: 2 (over x), fsdp: 4 (over z), ctx: 4 (over y, core).
Axes of the slice: x: 2, y: 2, z: 4, core: 2. Of those that a mesh axis runs over, the one named last changes fastest.
Arguments:
- inputs: bfloat16 [8, 1024, 2048], P(('rep', 'fsdp'), 'ctx'), may hold values from -6 to 6
- prefix: int32 [8], P(('rep', 'fsdp')), may hold values from 102 to 512
- joined_weight: bfloat16 [2048, 6144], P(('fsdp', 'ctx')), may hold values from -0.125 to 0.125
- query_bias: bfloat16 [2048], P(('fsdp', 'ctx')), may hold values from -3 to 3
- value_bias: bfloat16 [2048], P(('fsdp', 'ctx')), may hold values from -3 to 3
- dense_weight: bfloat16 [2048, 2048], P(('fsdp', 'ctx')), may hold values from -0.5 to 0.5
- dense_bias: bfloat16 [2048], P(('fsdp', 'ctx')), may hold values from -2 to 2
- expand_weight: bfloat16 [2048, 8192], P(('fsdp', 'ctx')), may hold values from -0.125 to 0.125
- expand_bias: bfloat16 [8192], P(('fsdp', 'ctx')), may hold values from -3 to 3
- shrink_weight: bfloat16 [8192, 2048], P(('fsdp', 'ctx')), may hold values from -0.0625 to 0.0625
- shrink_bias: bfloat16 [2048], P(('fsdp', 'ctx')), may hold values from -2 to 2
- first_gain: bfloat16 [2048], P(('fsdp', 'ctx')), may hold values from 0.5 to 1.5
- first_shift: bfloat16 [2048], P(('fsdp', 'ctx')), may hold values from -2 to 2
- second_gain: bfloat16 [2048], P(('fsdp', 'ctx')), may hold values from 0.5 to 1.5
- second_shift: bfloat16 [2048], P(('fsdp', 'ctx')), may hold values from -2 to 2
- cotangent: bfloat16 [8, 1024, 2048], P(('rep', 'fsdp'), 'ctx'), may hold values from -6 to 6
Outputs:
- layer_output: float32 [8, 1024, 2048], P(('rep', 'fsdp'), 'ctx')
- input_gradient: float32 [8, 1024, 2048], P(('rep', 'fsdp'), 'ctx')
- joined_gradient: float32 [2048, 6144], P(('fsdp', 'ctx'))
- query_bias_gradient: float32 [2048], P(('fsdp', 'ctx'))
- value_bias_gradient: float32 [2048], P(('fsdp', 'ctx'))
- dense_gradient: float32 [2048, 2048], P(('fsdp', 'ctx'))
- dense_bias_gradient: float32 [2048], P(('fsdp', 'ctx'))
- expand_gradient: float32 [2048, 8192], P(('fsdp', 'ctx'))
- expand_bias_gradient: float32 [8192], P(('fsdp', 'ctx'))
- shrink_gradient: float32 [8192, 2048], P(('fsdp', 'ctx'))
- shrink_bias_gradient: float32 [2048], P(('fsdp', 'ctx'))
- first_gain_gradient: float32 [2048], P(('fsdp', 'ctx'))
- first_shift_gradient: float32 [2048], P(('fsdp', 'ctx'))
- second_gain_gradient: float32 [2048], P(('fsdp', 'ctx'))
- second_shift_gradient: float32 [2048], P(('fsdp', 'ctx'))
All inputs are finite; a program needn't handle non-finite values.
Results may differ from a plain program's by a relative error of at most 0.014.
Values may be sent and summed in bfloat16 or wider, within the bound.
No kernel may reach another device: no remote copies, remote signals or barrier semaphores. Data moves between devices by JAX's collectives and lax.ppermute only.
A program may use at most 576 MiB of HBM per device.

v0:
```python
import jax
import jax.numpy as jnp
from jax import lax
from jax.sharding import PartitionSpec as P

H = 32
HD = 64


def layer_norm(values, gain, shift):
    average = jnp.mean(values, axis=-1, keepdims=True)
    centred = values - average
    variance = jnp.mean(centred * centred, axis=-1, keepdims=True)
    return centred * lax.rsqrt(variance + 1e-05) * gain + shift


def exact_gelu(values):
    return jax.nn.gelu(values, approximate=False)


def score_logits(query_heads, key_heads, prefix, first_place):
    raw = jnp.einsum("sqhe,skhe->shqk", query_heads, key_heads, preferred_element_type=jnp.float32)
    queries_here = query_heads.shape[1]
    length = key_heads.shape[1]
    heads = query_heads.shape[2]
    query_place = first_place + jnp.arange(queries_here, dtype=jnp.int32)
    key_place = jnp.arange(length, dtype=jnp.int32)
    distance = jnp.abs(query_place[:, None] - key_place[None, :]).astype(jnp.float32)
    allowed = (key_place[None, None, :] <= query_place[None, :, None]) | (
        key_place[None, None, :] < prefix[:, None, None]
    )
    order = jnp.arange(heads, dtype=jnp.int32).astype(jnp.float32)
    slopes = jnp.exp2(-8.0 * (order + 1.0) / heads)
    logits = raw * 0.125 - slopes[None, :, None, None] * distance[None, None]
    return (logits, allowed[:, None])


def shards(
    inputs,
    prefix,
    joined_weight,
    query_bias,
    value_bias,
    dense_weight,
    dense_bias,
    expand_weight,
    expand_bias,
    shrink_weight,
    shrink_bias,
    first_gain,
    first_shift,
    second_gain,
    second_shift,
    cotangent,
):
    sequences, span_rows, features = inputs.shape
    tokens = sequences * span_rows
    attn_parts = (
        lax.all_gather(joined_weight, ("fsdp", "ctx"), axis=0, tiled=True),
        lax.all_gather(query_bias, ("fsdp", "ctx"), axis=0, tiled=True),
        lax.all_gather(value_bias, ("fsdp", "ctx"), axis=0, tiled=True),
        lax.all_gather(dense_weight, ("fsdp", "ctx"), axis=0, tiled=True),
        lax.all_gather(dense_bias, ("fsdp", "ctx"), axis=0, tiled=True),
        lax.all_gather(first_gain, ("fsdp", "ctx"), axis=0, tiled=True),
        lax.all_gather(first_shift, ("fsdp", "ctx"), axis=0, tiled=True),
    )
    joined_all, qbias_all, vbias_all, dense_all, dbias_all, gain_one, shift_one = attn_parts
    start = inputs.astype(jnp.float32).reshape(tokens, features)
    gain_first = gain_one.astype(jnp.float32)
    shift_first = shift_one.astype(jnp.float32)
    normed = layer_norm(start, gain_first, shift_first).astype(jnp.bfloat16)
    projected = jnp.dot(normed, joined_all, preferred_element_type=jnp.float32)
    queries = (projected[:, :features] + qbias_all.astype(jnp.float32)).astype(jnp.bfloat16)
    keys_own = projected[:, features : 2 * features].astype(jnp.bfloat16)
    values_own = (projected[:, 2 * features :] + vbias_all.astype(jnp.float32)).astype(jnp.bfloat16)
    keys_all, values_all = (
        lax.all_gather(keys_own.reshape(sequences, span_rows, features), "ctx", axis=1, tiled=True),
        lax.all_gather(
            values_own.reshape(sequences, span_rows, features), "ctx", axis=1, tiled=True
        ),
    )
    length = keys_all.shape[1]
    query_heads = queries.reshape(sequences, span_rows, H, HD)
    key_heads = keys_all.reshape(sequences, length, H, HD)
    value_heads = values_all.reshape(sequences, length, H, HD)
    first_place = lax.axis_index("ctx") * span_rows
    logits, allowed = score_logits(query_heads, key_heads, prefix, first_place)
    masked = jnp.where(allowed, logits, -1e30)
    largest = jnp.max(masked, axis=-1, keepdims=True)
    exponent = jnp.exp(masked - largest)
    totals = jnp.sum(exponent, axis=-1, keepdims=True)
    log_total = largest + jnp.log(totals)
    probs_low = (exponent / totals).astype(jnp.bfloat16)
    mixture = jnp.einsum(
        "shqk,skhe->sqhe", probs_low, value_heads, preferred_element_type=jnp.float32
    )
    attended = mixture.reshape(tokens, features).astype(jnp.bfloat16)
    midway = (
        start
        + jnp.dot(attended, dense_all, preferred_element_type=jnp.float32)
        + dbias_all.astype(jnp.float32)
    )
    mlp_parts = (
        lax.all_gather(expand_weight, ("fsdp", "ctx"), axis=0, tiled=True),
        lax.all_gather(expand_bias, ("fsdp", "ctx"), axis=0, tiled=True),
        lax.all_gather(shrink_weight, ("fsdp", "ctx"), axis=0, tiled=True),
        lax.all_gather(shrink_bias, ("fsdp", "ctx"), axis=0, tiled=True),
        lax.all_gather(second_gain, ("fsdp", "ctx"), axis=0, tiled=True),
        lax.all_gather(second_shift, ("fsdp", "ctx"), axis=0, tiled=True),
    )
    expand_all, ebias_all, shrink_all, sbias_all, gain_two, shift_two = mlp_parts
    gain_second = gain_two.astype(jnp.float32)
    shift_second = shift_two.astype(jnp.float32)
    normed_two = layer_norm(midway, gain_second, shift_second).astype(jnp.bfloat16)
    expanded = jnp.dot(
        normed_two, expand_all, preferred_element_type=jnp.float32
    ) + ebias_all.astype(jnp.float32)
    activated = exact_gelu(expanded).astype(jnp.bfloat16)
    result = (
        midway
        + jnp.dot(activated, shrink_all, preferred_element_type=jnp.float32)
        + sbias_all.astype(jnp.float32)
    )
    again_mlp = (
        lax.all_gather(expand_weight, ("fsdp", "ctx"), axis=0, tiled=True),
        lax.all_gather(shrink_weight, ("fsdp", "ctx"), axis=0, tiled=True),
        lax.all_gather(second_gain, ("fsdp", "ctx"), axis=0, tiled=True),
    )
    back_expand, back_shrink = (again_mlp[0], again_mlp[1])
    back_gain_two = again_mlp[2].astype(jnp.float32)
    grad_out = cotangent.reshape(tokens, features)
    grad_out_float = grad_out.astype(jnp.float32)
    shrink_term = jnp.einsum("rf,rd->fd", activated, grad_out, preferred_element_type=jnp.float32)
    sbias_term = jnp.sum(grad_out_float, axis=0)
    d_activated = jnp.einsum("rd,fd->rf", grad_out, back_shrink, preferred_element_type=jnp.float32)
    d_expanded = jax.vjp(exact_gelu, expanded)[1](d_activated)[0].astype(jnp.bfloat16)
    expand_term = jnp.einsum(
        "rd,rf->df", normed_two, d_expanded, preferred_element_type=jnp.float32
    )
    ebias_term = jnp.sum(d_expanded.astype(jnp.float32), axis=0)
    d_normed_two = jnp.einsum(
        "rf,df->rd", d_expanded, back_expand, preferred_element_type=jnp.float32
    )
    norm_back_two = jax.vjp(layer_norm, midway, back_gain_two, shift_second)[1]
    d_mid_norm, gain_two_term, shift_two_term = norm_back_two(d_normed_two)
    d_midway = grad_out_float + d_mid_norm
    mlp_grads = (
        lax.psum_scatter(expand_term, ("fsdp", "ctx"), scatter_dimension=0, tiled=True),
        lax.psum_scatter(ebias_term, ("fsdp", "ctx"), scatter_dimension=0, tiled=True),
        lax.psum_scatter(shrink_term, ("fsdp", "ctx"), scatter_dimension=0, tiled=True),
        lax.psum_scatter(sbias_term, ("fsdp", "ctx"), scatter_dimension=0, tiled=True),
        lax.psum_scatter(gain_two_term, ("fsdp", "ctx"), scatter_dimension=0, tiled=True),
        lax.psum_scatter(shift_two_term, ("fsdp", "ctx"), scatter_dimension=0, tiled=True),
    )
    again_attn = (
        lax.all_gather(joined_weight, ("fsdp", "ctx"), axis=0, tiled=True),
        lax.all_gather(dense_weight, ("fsdp", "ctx"), axis=0, tiled=True),
        lax.all_gather(first_gain, ("fsdp", "ctx"), axis=0, tiled=True),
    )
    back_joined, back_dense = (again_attn[0], again_attn[1])
    back_gain_one = again_attn[2].astype(jnp.float32)
    d_attended_out = d_midway.astype(jnp.bfloat16)
    dense_term = jnp.einsum(
        "rd,re->de", attended, d_attended_out, preferred_element_type=jnp.float32
    )
    dbias_term = jnp.sum(d_attended_out.astype(jnp.float32), axis=0)
    d_attended = jnp.einsum(
        "re,de->rd", d_attended_out, back_dense, preferred_element_type=jnp.float32
    ).astype(jnp.bfloat16)
    d_heads = d_attended.reshape(sequences, span_rows, H, HD)
    logits_again, allowed_again = score_logits(query_heads, key_heads, prefix, first_place)
    probs = jnp.where(allowed_again, jnp.exp(logits_again - log_total), 0.0)
    probs_again = probs.astype(jnp.bfloat16)
    d_probs = jnp.einsum(
        "sqhe,skhe->shqk", d_heads, value_heads, preferred_element_type=jnp.float32
    )
    weighted = jnp.sum(probs * d_probs, axis=-1, keepdims=True)
    d_raw = (probs * (d_probs - weighted) * 0.125).astype(jnp.bfloat16)
    d_queries = jnp.einsum("shqk,skhe->sqhe", d_raw, key_heads, preferred_element_type=jnp.float32)
    d_keys_full = jnp.einsum(
        "shqk,sqhe->skhe", d_raw, query_heads, preferred_element_type=jnp.float32
    )
    d_values_full = jnp.einsum(
        "shqk,sqhe->skhe", probs_again, d_heads, preferred_element_type=jnp.float32
    )
    d_keys, d_values = (
        lax.psum_scatter(
            d_keys_full.reshape(sequences, length, features).astype(jnp.bfloat16),
            "ctx",
            scatter_dimension=1,
            tiled=True,
        ).astype(jnp.float32),
        lax.psum_scatter(
            d_values_full.reshape(sequences, length, features).astype(jnp.bfloat16),
            "ctx",
            scatter_dimension=1,
            tiled=True,
        ).astype(jnp.float32),
    )
    d_queries_low = d_queries.reshape(tokens, features).astype(jnp.bfloat16)
    d_keys_low = d_keys.reshape(tokens, features).astype(jnp.bfloat16)
    d_values_low = d_values.reshape(tokens, features).astype(jnp.bfloat16)
    qbias_term = jnp.sum(d_queries_low.astype(jnp.float32), axis=0)
    vbias_term = jnp.sum(d_values_low.astype(jnp.float32), axis=0)
    d_projected = jnp.concatenate([d_queries_low, d_keys_low, d_values_low], axis=1)
    joined_term = jnp.einsum("rd,re->de", normed, d_projected, preferred_element_type=jnp.float32)
    d_normed = jnp.einsum("re,de->rd", d_projected, back_joined, preferred_element_type=jnp.float32)
    norm_back_one = jax.vjp(layer_norm, start, back_gain_one, shift_first)[1]
    d_start_norm, gain_one_term, shift_one_term = norm_back_one(d_normed)
    input_gradient = d_midway + d_start_norm
    attn_grads = (
        lax.psum_scatter(joined_term, ("fsdp", "ctx"), scatter_dimension=0, tiled=True),
        lax.psum_scatter(qbias_term, ("fsdp", "ctx"), scatter_dimension=0, tiled=True),
        lax.psum_scatter(vbias_term, ("fsdp", "ctx"), scatter_dimension=0, tiled=True),
        lax.psum_scatter(dense_term, ("fsdp", "ctx"), scatter_dimension=0, tiled=True),
        lax.psum_scatter(dbias_term, ("fsdp", "ctx"), scatter_dimension=0, tiled=True),
        lax.psum_scatter(gain_one_term, ("fsdp", "ctx"), scatter_dimension=0, tiled=True),
        lax.psum_scatter(shift_one_term, ("fsdp", "ctx"), scatter_dimension=0, tiled=True),
    )
    summed = (
        lax.psum(attn_grads[0].astype(jnp.bfloat16), "rep").astype(jnp.float32),
        lax.psum(attn_grads[1].astype(jnp.bfloat16), "rep").astype(jnp.float32),
        lax.psum(attn_grads[2].astype(jnp.bfloat16), "rep").astype(jnp.float32),
        lax.psum(attn_grads[3].astype(jnp.bfloat16), "rep").astype(jnp.float32),
        lax.psum(attn_grads[4].astype(jnp.bfloat16), "rep").astype(jnp.float32),
        lax.psum(attn_grads[5].astype(jnp.bfloat16), "rep").astype(jnp.float32),
        lax.psum(attn_grads[6].astype(jnp.bfloat16), "rep").astype(jnp.float32),
        lax.psum(mlp_grads[0].astype(jnp.bfloat16), "rep").astype(jnp.float32),
        lax.psum(mlp_grads[1].astype(jnp.bfloat16), "rep").astype(jnp.float32),
        lax.psum(mlp_grads[2].astype(jnp.bfloat16), "rep").astype(jnp.float32),
        lax.psum(mlp_grads[3].astype(jnp.bfloat16), "rep").astype(jnp.float32),
        lax.psum(mlp_grads[4].astype(jnp.bfloat16), "rep").astype(jnp.float32),
        lax.psum(mlp_grads[5].astype(jnp.bfloat16), "rep").astype(jnp.float32),
    )
    attn_grads = summed[:7]
    mlp_grads = summed[7:]
    return (
        result.reshape(sequences, span_rows, features),
        input_gradient.reshape(sequences, span_rows, features),
        attn_grads[0],
        attn_grads[1],
        attn_grads[2],
        attn_grads[3],
        attn_grads[4],
        mlp_grads[0],
        mlp_grads[1],
        mlp_grads[2],
        mlp_grads[3],
        attn_grads[5],
        attn_grads[6],
        mlp_grads[4],
        mlp_grads[5],
    )


def solution(mesh):
    in_specs = (
        P(("rep", "fsdp"), "ctx", None),
        P(("rep", "fsdp")),
        P(("fsdp", "ctx"), None),
        P(("fsdp", "ctx")),
        P(("fsdp", "ctx")),
        P(("fsdp", "ctx"), None),
        P(("fsdp", "ctx")),
        P(("fsdp", "ctx"), None),
        P(("fsdp", "ctx")),
        P(("fsdp", "ctx"), None),
        P(("fsdp", "ctx")),
        P(("fsdp", "ctx")),
        P(("fsdp", "ctx")),
        P(("fsdp", "ctx")),
        P(("fsdp", "ctx")),
        P(("rep", "fsdp"), "ctx", None),
    )
    out_specs = (
        P(("rep", "fsdp"), "ctx", None),
        P(("rep", "fsdp"), "ctx", None),
        P(("fsdp", "ctx"), None),
        P(("fsdp", "ctx")),
        P(("fsdp", "ctx")),
        P(("fsdp", "ctx"), None),
        P(("fsdp", "ctx")),
        P(("fsdp", "ctx"), None),
        P(("fsdp", "ctx")),
        P(("fsdp", "ctx"), None),
        P(("fsdp", "ctx")),
        P(("fsdp", "ctx")),
        P(("fsdp", "ctx")),
        P(("fsdp", "ctx")),
        P(("fsdp", "ctx")),
    )
    return jax.shard_map(shards, mesh=mesh, in_specs=in_specs, out_specs=out_specs, check_vma=False)
```

profile of v0, /device:TPU:0, one launch (start us, length us, event | category | flops | bytes accessed | tf_op | source)
XLA Modules:
  0.0 2958.1 jit_solution(15318190174671491095)
XLA Ops:
  8.0 23.2 all-gather.5
  48.7 18.9 all-gather.2
  88.3 52.7 %all-gather.18.cloned.1.call-done = bf16[2048,6144]{1,0:T(8,128)(2,1)} async-done(((bf16[128,6144]{1,0:T(8,128)(2,1)}), bf16[2048,6144]{1,0:T(8,128)(2,1)}) %all-gather.18.cloned.1.call-update) | async-done | bytes 25165840 | tf_op jit(solution)/shard_map/all_gather | solution.py:59
  162.6 20.3 all-gather.6
  200.3 18.7 all-gather.8
  251.9 18.6 select_reduce_fusion
  312.7 161.2 %all-gather.22.cloned.1.call-done = bf16[2048,8192]{1,0:T(8,128)(2,1)} async-done(((bf16[128,8192]{1,0:T(8,128)(2,1)}), bf16[2048,8192]{1,0:T(8,128)(2,1)}) %all-gather.22.cloned.1.call-update) | async-done | bytes 33554448 | tf_op jit(solution)/shard_map/all_gather | solution.py:104
  473.8 20.0 convolution_add_fusion
  493.8 149.6 %all-gather.24.cloned.1.call-done = bf16[8192,2048]{1,0:T(8,128)(2,1)} async-done(((bf16[512,2048]{1,0:T(8,128)(2,1)}), bf16[8192,2048]{1,0:T(8,128)(2,1)}) %all-gather.24.cloned.1.call-update) | async-done | bytes 33554448 | tf_op jit(solution)/shard_map/all_gather | solution.py:106
  643.4 33.6 %convert_reduce_fusion = (f32[8192]{0:T(1024)}, bf16[256,8192]{1,0:T(8,128)(2,1)}) fusion(f32[256,8192]{1,0:T(8,128)} %convolution_add_fusion, bf16[8192,2048]{1,0:T(8,128)(2,1)} %all-gather.24.cloned.1.call-done, bf16[1,256,2048]{2,1,0:T(8,128)(2,1)S(1)} %copy-done.10), kind=kOutput, calls=%fused_computation.24 | convolution fusion | flops 8745115648 | bytes 47218688 | tf_op jit(solution)/shard_map/rd,fd->rf/dot_general | solution.py:135
  677.0 18.4 multiply_reduce_fusion.1
  741.0 61.5 %fusion.27 = bf16[32,64,1024]{2,1,0:T(8,128)(2,1)} fusion(bf16[256,32,64]{0,2,1:T(8,128)(2,1)} %bitcast.141, f32[32,256,1024]{2,1,0:T(8,128)} %fusion.88, f32[32,256,1024]{2,1,0:T(8,128)} %get-tuple-element.53, f32[32,256]{1,0:T(8,128)S(1)} %log_add_fusion, pred[256,1024]{1,0:T(8,128)(4,1)S(1)} %fusion.64), kind=kOutput, calls=%fused_computation.43 | convolution fusion | flops 1151345664 | bytes 72646656 | tf_op jit(solution)/shard_map/shqk,sqhe->skhe/dot_general | solution.py:180
  812.4 61.6 %convert_reduce_fusion.5 = (f32[32,64]{1,0:T(8,128)}, bf16[32,64,256]{2,1,0:T(8,128)(2,1)S(1)}) fusion(bf16[1024,32,64]{0,2,1:T(8,128)(2,1)} %bitcast.134, f32[32,256,1024]{2,1,0:T(8,128)} %fusion.88, f32[32,256,1024]{2,1,0:T(8,128)} %get-tuple-element.53, f32[32,256]{1,0:T(8,128)S(1)} %log_add_fusion, pred[256,1024]{1,0:T(8,128)(4,1)S(1)} %fusion.64), kind=kOutput, calls=%fused_computation.75 | convolution fusion | flops 1150819328 | bytes 72654848 | tf_op jit(solution)/shard_map/shqk,skhe->sqhe/dot_general | solution.py:179
  874.0 20.7 fusion.56
  894.8 34.3 %fusion.58 = f32[8192,2048]{1,0:T(8,128)} fusion(bf16[1,256,2048]{2,1,0:T(8,128)(2,1)S(1)} %copy-done.10, f32[256,8192]{1,0:T(8,128)} %convolution_add_fusion), kind=kOutput, calls=%fused_computation.85 | convolution fusion | flops 8726249472 | bytes 76546048 | tf_op jit(solution)/shard_map/rf,rd->fd/dot_general | solution.py:133
  930.8 26.1 fusion.81
  959.4 20.2 all-gather.10
  979.7 50.7 %reduce-scatter.13.cloned.1.call-done = f32[128,2048]{1,0:T(8,128)} async-done(((f32[2048,2048]{1,0:T(8,128)}), f32[128,2048]{1,0:T(8,128)}) %reduce-scatter.13.cloned.1.call-update) | async-done | bytes 1048592 | tf_op jit(solution)/shard_map/reduce_scatter | solution.py:215
  1032.5 468.8 %reduce-scatter.11.cloned.1.call-done = f32[128,6144]{1,0:T(8,128)} async-done(((f32[2048,6144]{1,0:T(8,128)}), f32[128,6144]{1,0:T(8,128)}) %reduce-scatter.11.cloned.1.call-update) | async-done | bytes 3145744 | tf_op jit(solution)/shard_map/reduce_scatter | solution.py:212
  1504.5 637.2 %reduce-scatter.17.cloned.1.call-done = f32[512,2048]{1,0:T(8,128)} async-done(((f32[8192,2048]{1,0:T(8,128)}), f32[512,2048]{1,0:T(8,128)}) %reduce-scatter.17.cloned.1.call-update) | async-done | bytes 4194320 | tf_op jit(solution)/shard_map/reduce_scatter | solution.py:150
  2145.5 636.3 %reduce-scatter.15.cloned.1.call-done = f32[128,8192]{1,0:T(8,128)} async-done(((f32[2048,8192]{1,0:T(8,128)}), f32[128,8192]{1,0:T(8,128)}) %reduce-scatter.15.cloned.1.call-update) | async-done | bytes 4194320 | tf_op jit(solution)/shard_map/reduce_scatter | solution.py:148
  2785.6 31.8 %fusion.40 = f32[1,256,2048]{2,1,0:T(8,128)} fusion(f32[256,2048]{1,0:T(8,128)S(1)} %copy-done.4, bf16[8192,2048]{1,0:T(8,128)(2,1)} %all-gather.24.cloned.1.call-done, f32[2048]{0:T(1024)S(1)} %bitcast.159, f32[256,8192]{1,0:T(8,128)} %convolution_add_fusion), kind=kOutput, calls=%fused_computation.57 | convolution fusion | flops 8727298048 | bytes 46145536 | tf_op jit(solution)/shard_map/dot_general | solution.py:121
  2837.4 60.8 %all-reduce.9 = (bf16[2048]{0:T(1024)(128)(2,1)S(1)}, bf16[2048]{0:T(1024)(128)(2,1)S(1)}, bf16[2048]{0:T(1024)(128)(2,1)S(1)}, bf16[8192]{0:T(1024)(128)(2,1)S(...) all-reduce(f32[2048]{0:T(1024)S(1)} %reduce_sum.189, ...), channel_id=7, replica_groups=mesh['rep'=2,'fsdp'=4,'ctx'=4] {'fsdp','ctx'}, use_global_device_ids=true, to_apply=%region_16.17.clone | all-reduce | flops 24576 | bytes 147456
  2908.7 30.4 %all-reduce.14.cloned.1.call-done = (bf16[128,6144]{1,0:T(8,128)(2,1)}, bf16[128,2048]{1,0:T(8,128)(2,1)}, bf16[128,8192]{1,0:T(8,128)(2,1)}, bf16[512,2048]{1,0:T(8,128)(2,1)}) async-done(((bf16[128,6144]{1,0:T(8,128)(2,1)}, bf16[128,2048]{1,0:T(8,128)(2,1)}, bf16[128,8192]{1,0:T(8,128)(2,1)}, bf16[512,2048]{1,0:T(8,128)(2,1)}), (bf16[128,6144]{1,0:T(8,128)(2,1)}, bf16[128,2048]{1,0:T(8,128)(2,1)}, ...) | async-done | bytes 6291472 | tf_op jit(solution)/shard_map/psum | solution.py:221
  (209 shorter events, 265.8 us)
Async XLA Ops:
  7.2 133.9 %all-gather.18.cloned.1.call-start = ((), (), s32[]{:S(2)}) async-start(), calls=%async_computation.6 | async-start | bytes 26738688 | tf_op jit(solution)/shard_map/all_gather | solution.py:59
  7.9 230.8 %all-gather.26.cloned.1.call-start = ((), (), s32[]{:S(2)}) async-start(), calls=%async_computation.16 | async-start | bytes 5242880 | tf_op jit(solution)/shard_map/all_gather | solution.py:78
  67.6 85.6 %copy-start.15 = (f32[16,1,128]{2,1,0:T(1,128)}, f32[16,1,128]{2,1,0:T(1,128)S(1)}, u32[]{:S(2)}) copy-start(f32[16,1,128]{2,1,0:T(1,128)S(1)} %convert_element_type.330) | copy-start | bytes 24580
  85.1 68.0 %copy-start.18 = (f32[16,1,128]{2,1,0:T(1,128)}, f32[16,1,128]{2,1,0:T(1,128)S(1)}, u32[]{:S(2)}) copy-start(f32[16,1,128]{2,1,0:T(1,128)S(1)} %convert_element_type.331) | copy-start | bytes 24580
  86.6 66.5 %copy-start.24 = (f32[256]{0:T(256)}, f32[256]{0:T(256)S(1)}, u32[]{:S(2)}) copy-start(f32[256]{0:T(256)S(1)} %broadcast_multiply_fusion.1) | copy-start | bytes 3076
  88.3 64.8 %copy-start.39 = (f32[256]{0:T(256)}, f32[256]{0:T(256)S(1)}, u32[]{:S(2)}) copy-start(f32[256]{0:T(256)S(1)} %fusion.47) | copy-start | bytes 3076
  88.3 64.8 %copy-start.27 = (f32[256]{0:T(256)}, f32[256]{0:T(256)S(1)}, u32[]{:S(2)}) copy-start(f32[256]{0:T(256)S(1)} %fusion.65) | copy-start | bytes 3076
  157.3 88.2 %all-gather.28.cloned.1.call-start = ((), (), s32[]{:S(2)}) async-start(), calls=%async_computation.17 | async-start | bytes 5242880 | tf_op jit(solution)/shard_map/all_gather | solution.py:77
  160.1 145.9 %all-gather.20.cloned.1.call-start = ((), (), s32[]{:S(2)}) async-start(), calls=%async_computation.7 | async-start | bytes 8912896 | tf_op jit(solution)/shard_map/all_gather | solution.py:62
  160.7 313.2 %all-gather.22.cloned.1.call-start = ((), (), s32[]{:S(2)}) async-start(), calls=%async_computation.8 | async-start | bytes 35651584 | tf_op jit(solution)/shard_map/all_gather | solution.py:104
  161.3 482.1 %all-gather.24.cloned.1.call-start = ((), (), s32[]{:S(2)}) async-start(), calls=%async_computation.9 | async-start | bytes 35651584 | tf_op jit(solution)/shard_map/all_gather | solution.py:106
  161.8 712.1 %reduce-scatter.9.cloned.1.call-start = ((), (), s32[]{:S(2)}) async-start(), calls=%async_computation.11 | async-start | bytes 5242880 | tf_op jit(solution)/shard_map/reduce_scatter | solution.py:193
  200.2 495.1 %copy-start.20 = (f32[16,1,128]{2,1,0:T(1,128)}, f32[16,1,128]{2,1,0:T(1,128)S(1)}, u32[]{:S(2)}) copy-start(f32[16,1,128]{2,1,0:T(1,128)S(1)} %convert_element_type.335) | copy-start | bytes 24580
  219.0 254.8 %copy-start.22 = (f32[16,1,128]{2,1,0:T(1,128)}, f32[16,1,128]{2,1,0:T(1,128)S(1)}, u32[]{:S(2)}) copy-start(f32[16,1,128]{2,1,0:T(1,128)S(1)} %convert_element_type.336) | copy-start | bytes 24580
  312.2 383.1 %copy-start.3 = (f32[256,2048]{1,0:T(8,128)}, f32[256,2048]{1,0:T(8,128)S(1)}, u32[]{:S(2)}) copy-start(f32[256,2048]{1,0:T(8,128)S(1)} %get-tuple-element.55) | copy-start | bytes 6291460
  312.2 383.1 %copy-start.30 = (f32[256]{0:T(256)}, f32[256]{0:T(256)S(1)}, u32[]{:S(2)}) copy-start(f32[256]{0:T(256)S(1)} %broadcast_multiply_fusion) | copy-start | bytes 3076
  312.6 382.8 %copy-start.32 = (f32[256]{0:T(256)}, f32[256]{0:T(256)S(1)}, u32[]{:S(2)}) copy-start(f32[256]{0:T(256)S(1)} %fusion.66) | copy-start | bytes 3076
  473.8 169.6 %copy-start.10 = (bf16[1,256,2048]{2,1,0:T(8,128)(2,1)S(1)}, bf16[1,256,2048]{2,1,0:T(8,128)(2,1)}, u32[]{:S(2)}) copy-start(bf16[1,256,2048]{2,1,0:T(8,128)(2,1)} %param.31) | copy-start | bytes 3145732
  723.7 150.3 %reduce-scatter.7.cloned.1.call-start = ((), (), s32[]{:S(2)}) async-start(), calls=%async_computation.10 | async-start | bytes 5242880 | tf_op jit(solution)/shard_map/reduce_scatter | solution.py:187
  802.5 227.9 %reduce-scatter.13.cloned.1.call-start = ((), (), s32[]{:S(2)}) async-start(), calls=%async_computation.13 | async-start | bytes 17825792 | tf_op jit(solution)/shard_map/reduce_scatter | solution.py:215
  812.3 688.9 %reduce-scatter.11.cloned.1.call-start = ((), (), s32[]{:S(2)}) async-start(), calls=%async_computation.12 | async-start | bytes 53477376 | tf_op jit(solution)/shard_map/reduce_scatter | solution.py:212
  894.8 1246.9 %reduce-scatter.17.cloned.1.call-start = ((), (), s32[]{:S(2)}) async-start(), calls=%async_computation.15 | async-start | bytes 71303168 | tf_op jit(solution)/shard_map/reduce_scatter | solution.py:150
  929.2 1852.5 %reduce-scatter.15.cloned.1.call-start = ((), (), s32[]{:S(2)}) async-start(), calls=%async_computation.14 | async-start | bytes 71303168 | tf_op jit(solution)/shard_map/reduce_scatter | solution.py:148
  956.9 1982.2 %all-reduce.14.cloned.1.call-start = ((), (), s32[]{:S(2)}) async-start(), calls=%async_computation.18 | async-start | bytes 12582912 | tf_op jit(solution)/shard_map/psum | solution.py:221
  (38 other events, 792.9 us)
Sparse Core Ops, SparseCore 0:
  9.6 131.3 all-gather.17
  157.4 34.7 all-gather.25
  194.3 34.7 all-gather.27
  231.1 74.8 all-gather.19
  307.5 166.2 all-gather.21
  475.3 168.0 all-gather.23
  723.8 44.4 reduce-scatter.8
  802.6 44.8 reduce-scatter.6
  851.6 178.7 reduce-scatter.12
  1034.5 466.7 reduce-scatter.10
  1505.5 636.1 reduce-scatter.16
  2145.8 635.9 reduce-scatter.14
  2785.7 153.4 all-reduce.13
where the time goes:
time: 2960 us
  waiting for transfers between devices  2190 us (74%)
  matrix products  424 us (14%)
  blocking collectives  238 us (8%)
  other arithmetic  59.3 us (2%)
    reduce_scatter x1, waiting for transfers between devices, shards(): lax.psum_scatter(shrink_term, ('fsdp', 'ctx'), scatter_dimension=0, tiled...  637 us
    reduce_scatter x1, waiting for transfers between devices, shards(): lax.psum_scatter(expand_term, ('fsdp', 'ctx'), scatter_dimension=0, tiled...  636 us
    reduce_scatter x1, waiting for transfers between devices, shards(): lax.psum_scatter(joined_term, ('fsdp', 'ctx'), scatter_dimension=0, tiled...  469 us
    all_gather x1, waiting for transfers between devices, shards(): lax.all_gather(expand_weight, ('fsdp', 'ctx'), axis=0, tiled=True)  161 us
    all_gather x1, waiting for transfers between devices, shards(): lax.all_gather(shrink_weight, ('fsdp', 'ctx'), axis=0, tiled=True)  150 us
    dot_general x1, matrix products, shards(): jnp.einsum('shqk,skhe->sqhe', d_raw, key_heads, preferred_element_type=jn...  61.6 us
    dot_general x1, matrix products, shards(): jnp.einsum('shqk,sqhe->skhe', d_raw, query_heads, preferred_element_type=...  61.5 us
    unnamed x1, blocking collectives  60.8 us
  transfers between devices with their start and end apart: 13, of which 9 were waited for; matrix products, arithmetic and copies ran while one was open for 13% of the time, Pallas kernels for 0%

commit v1 on v0

--- a/solution.py
+++ b/solution.py
@@ -5,6 +5,18 @@
 
 H = 32
 HD = 64
+
+
+def gather_by_bits(x, axis, dim):
+    ways, here, turn = (lax.axis_size(axis), lax.axis_index(axis), x.shape[dim])
+    line, have = (x, 1)
+    while have < ways:
+        line = jnp.concatenate(
+            [line, lax.ppermute(line, axis, [(d, (d - have) % ways) for d in range(ways)])],
+            axis=dim,
+        )
+        have = 2 * have
+    return jnp.roll(line, here * turn, axis=dim)
 
 
 def layer_norm(values, gain, shift):
@@ -103,7 +115,7 @@
     mlp_parts = (
         lax.all_gather(expand_weight, ("fsdp", "ctx"), axis=0, tiled=True),
         lax.all_gather(expand_bias, ("fsdp", "ctx"), axis=0, tiled=True),
-        lax.all_gather(shrink_weight, ("fsdp", "ctx"), axis=0, tiled=True),
+        gather_by_bits(shrink_weight, ("fsdp", "ctx"), 0),
         lax.all_gather(shrink_bias, ("fsdp", "ctx"), axis=0, tiled=True),
         lax.all_gather(second_gain, ("fsdp", "ctx"), axis=0, tiled=True),
         lax.all_gather(second_shift, ("fsdp", "ctx"), axis=0, tiled=True),

time: 2960 us -> 3700 us (1.25)
  blocking collectives: 238 us -> 620 us
  waiting for transfers between devices: 2190 us -> 2470 us
  local copies, waits for them, and re-layouts: 25.4 us -> 85.5 us
    ppermute x0 -> x4, waiting for transfers between devices: none -> 1040 us  [gather_by_bits(): lax.ppermute(line, axis, [(d, (d - have) % ways) for d in range(ways)])]
    reduce_scatter x1, waiting for transfers between devices: 469 us -> 0.01 us  [shards(): lax.psum_scatter(joined_term, ('fsdp', 'ctx'), scatter_dimension=0, tiled...]
    all_gather x1, blocking collectives: 20.2 us -> 403 us  [shards(): lax.all_gather(shrink_bias, ('fsdp', 'ctx'), axis=0, tiled=True)]
    reduce_scatter x1, waiting for transfers between devices: 636 us -> 386 us  [shards(): lax.psum_scatter(expand_term, ('fsdp', 'ctx'), scatter_dimension=0, tiled...]
    reduce_scatter x1, waiting for transfers between devices: 50.7 us -> 0.01 us  [shards(): lax.psum_scatter(dense_term, ('fsdp', 'ctx'), scatter_dimension=0, tiled=...]
    unnamed x109 -> x132, local copies, waits for them, and re-layouts: 7.47 us -> 54.9 us
  transfers between devices with their start and end apart: 13 -> 17, of which waited for: 9 -> 11; matrix products, arithmetic and copies ran while one was open for 13% -> 11% of each run, Pallas kernels for 0% -> 0%
where the time goes in v1:
time: 3700 us
  waiting for transfers between devices  2470 us (67%)
  blocking collectives  620 us (17%)
  matrix products  430 us (12%)
  local copies, waits for them, and re-layouts  85.5 us (2%)
  other arithmetic  72.5 us (2%)
    ppermute x4, waiting for transfers between devices, gather_by_bits(): lax.ppermute(line, axis, [(d, (d - have) % ways) for d in range(ways)])  1040 us
    reduce_scatter x1, waiting for transfers between devices, shards(): lax.psum_scatter(shrink_term, ('fsdp', 'ctx'), scatter_dimension=0, tiled...  637 us
    all_gather x1, blocking collectives, shards(): lax.all_gather(shrink_bias, ('fsdp', 'ctx'), axis=0, tiled=True)  403 us
    reduce_scatter x1, waiting for transfers between devices, shards(): lax.psum_scatter(expand_term, ('fsdp', 'ctx'), scatter_dimension=0, tiled...  386 us
    all_gather x1, waiting for transfers between devices, shards(): lax.all_gather(shrink_weight, ('fsdp', 'ctx'), axis=0, tiled=True)  150 us
    all_gather x1, waiting for transfers between devices, shards(): lax.all_gather(expand_weight, ('fsdp', 'ctx'), axis=0, tiled=True)  131 us
    all_gather x1, waiting for transfers between devices, shards(): lax.all_gather(joined_weight, ('fsdp', 'ctx'), axis=0, tiled=True)  88.6 us
  transfers between devices with their start and end apart: 17, of which 11 were waited for; matrix products, arithmetic and copies ran while one was open for 11% of the time, Pallas kernels for 0%

profile of v1, /device:TPU:0, one launch (start us, length us, event | category | flops | bytes accessed | tf_op | source)
XLA Modules:
  0.0 3698.7 jit_solution(6269643087195217235)
XLA Ops:
  8.0 23.2 all-gather.2
  52.4 88.6 %all-gather.18.cloned.1.call-done = bf16[2048,6144]{1,0:T(8,128)(2,1)} async-done(((bf16[128,6144]{1,0:T(8,128)(2,1)}), bf16[2048,6144]{1,0:T(8,128)(2,1)}) %all-gather.18.cloned.1.call-update) | async-done | bytes 25165840 | tf_op jit(solution)/shard_map/all_gather | solution.py:71
  157.0 20.3 all-gather.5
  200.8 18.7 all-gather.6
  236.9 18.9 all-gather.8
  345.2 131.1 %all-gather.22.cloned.1.call-done = bf16[2048,8192]{1,0:T(8,128)(2,1)} async-done(((bf16[128,8192]{1,0:T(8,128)(2,1)}), bf16[2048,8192]{1,0:T(8,128)(2,1)}) %all-gather.22.cloned.1.call-update) | async-done | bytes 33554448 | tf_op jit(solution)/shard_map/all_gather | solution.py:116
  476.4 20.0 convolution_add_fusion
  496.4 149.5 %all-gather.24.cloned.1.call-done = bf16[8192,2048]{1,0:T(8,128)(2,1)} async-done(((bf16[512,2048]{1,0:T(8,128)(2,1)}), bf16[8192,2048]{1,0:T(8,128)(2,1)}) %all-gather.24.cloned.1.call-update) | async-done | bytes 33554448 | tf_op jit(solution)/shard_map/all_gather | solution.py:138
  645.9 33.5 convert_reduce_fusion
  727.2 60.9 %fusion.29 = bf16[32,64,1024]{2,1,0:T(8,128)(2,1)} fusion(bf16[256,32,64]{0,2,1:T(8,128)(2,1)} %bitcast.140, f32[32,256,1024]{2,1,0:T(8,128)} %fusion.98, f32[32,256,1024]{2,1,0:T(8,128)} %get-tuple-element.53, f32[32,256]{1,0:T(8,128)S(1)} %copy-done.35, pred[256,1024]{1,0:T(8,128)(4,1)S(1)} %copy-done.21), kind=kOutput, calls=%fused_computation.48 | convolution fusion | flops 1151345664 | bytes 72646656 | tf_op jit(solution)/shard_map/shqk,sqhe->skhe/dot_general | solution.py:192
  815.8 61.3 %convert_reduce_fusion.5 = (f32[32,64]{1,0:T(8,128)}, bf16[32,64,256]{2,1,0:T(8,128)(2,1)}) fusion(bf16[1024,32,64]{0,2,1:T(8,128)(2,1)} %bitcast.133, f32[32,256,1024]{2,1,0:T(8,128)} %fusion.98, f32[32,256,1024]{2,1,0:T(8,128)} %get-tuple-element.53, f32[32,256]{1,0:T(8,128)S(1)} %copy-done.35, pred[256,1024]{1,0:T(8,128)(4,1)S(1)} %copy-done.21), kind=kOutput, calls=%fused_computation.80 | convolution fusion | flops 1150819328 | bytes 72654848 | tf_op jit(solution)/shard_map/shqk,skhe->sqhe/dot_general | solution.py:191
  880.7 26.0 fusion.65
  907.4 27.1 fusion.91
  935.7 34.3 fusion.67
  973.6 38.3 %collective-permute-done = bf16[512,2048]{1,0:T(8,128)(2,1)S(1)} collective-permute-done((bf16[512,2048]{1,0:T(8,128)(2,1)S(1)}, bf16[512,2048]{1,0:T(8,128)(2,1)S(1)}, u32[]{:S(2)}, u32[]{:S(2)}) %collective-permute-start) | collective-permute-done | bytes 2097184 | tf_op jit(solution)/shard_map/ppermute | solution.py:15
  1012.6 93.4 %collective-permute-done.1 = bf16[1024,2048]{1,0:T(8,128)(2,1)S(1)} collective-permute-done((bf16[1024,2048]{1,0:T(8,128)(2,1)S(1)}, bf16[1024,2048]{1,0:T(8,128)(2,1)S(1)}, u32[]{:S(2)}, u32[]{:S(2)}) %collective-permute-start.1) | collective-permute-done | bytes 4194336 | tf_op jit(solution)/shard_map/ppermute | solution.py:15
  1110.2 284.3 %collective-permute-done.2 = bf16[2048,2048]{1,0:T(8,128)(2,1)S(1)} collective-permute-done((bf16[2048,2048]{1,0:T(8,128)(2,1)S(1)}, bf16[2048,2048]{1,0:T(8,128)(2,1)S(1)}, u32[]{:S(2)}, u32[]{:S(2)}) %collective-permute-start.2) | collective-permute-done | bytes 8388640 | tf_op jit(solution)/shard_map/ppermute | solution.py:15
  1405.3 403.5 %all-gather.10 = bf16[16,1,128]{2,1,0:T(2,128)(2,1)S(1)} all-gather(bf16[1,1,128]{2,1,0:T(2,128)(2,1)S(1)} %bitcast.166), channel_id=1, replica_groups=mesh['rep'=2,'fsdp'=4,'ctx'=4] {'fsdp','ctx'}, dimensions={0}, use_global_device_ids=true | all-gather | bytes 4352 | tf_op jit(solution)/shard_map/all_gather | solution.py:119
  1824.6 623.4 %collective-permute-done.3 = bf16[4096,2048]{1,0:T(8,128)(2,1)} collective-permute-done((bf16[4096,2048]{1,0:T(8,128)(2,1)}, bf16[4096,2048]{1,0:T(8,128)(2,1)}, u32[]{:S(2)}, u32[]{:S(2)}) %collective-permute-start.3) | collective-permute-done | bytes 16777248 | tf_op jit(solution)/shard_map/ppermute | solution.py:15
  2496.5 386.3 %reduce-scatter.15.cloned.1.call-done = f32[128,8192]{1,0:T(8,128)} async-done(((f32[2048,8192]{1,0:T(8,128)}), f32[128,8192]{1,0:T(8,128)}) %reduce-scatter.15.cloned.1.call-update) | async-done | bytes 4194320 | tf_op jit(solution)/shard_map/reduce_scatter | solution.py:160
  2886.6 636.5 %reduce-scatter.17.cloned.1.call-done = f32[512,2048]{1,0:T(8,128)} async-done(((f32[8192,2048]{1,0:T(8,128)}), f32[512,2048]{1,0:T(8,128)}) %reduce-scatter.17.cloned.1.call-update) | async-done | bytes 4194320 | tf_op jit(solution)/shard_map/reduce_scatter | solution.py:162
  3527.0 31.6 fusion.48
  3578.9 60.7 %all-reduce.9 = (bf16[2048]{0:T(1024)(128)(2,1)S(1)}, bf16[2048]{0:T(1024)(128)(2,1)S(1)}, bf16[2048]{0:T(1024)(128)(2,1)S(1)}, bf16[8192]{0:T(1024)(128)(2,1)S(...) all-reduce(f32[2048]{0:T(1024)S(1)} %reduce_sum.189, ...), channel_id=7, replica_groups=mesh['rep'=2,'fsdp'=4,'ctx'=4] {'fsdp','ctx'}, use_global_device_ids=true, to_apply=%region_16.17.clone | all-reduce | flops 24576 | bytes 147456
  3650.1 30.5 all-reduce.14.cloned.1.call-done
  (244 shorter events, 379.8 us)
Async XLA Ops:
  7.2 133.8 %all-gather.18.cloned.1.call-start = ((), (), s32[]{:S(2)}) async-start(), calls=%async_computation.6 | async-start | bytes 26738688 | tf_op jit(solution)/shard_map/all_gather | solution.py:71
  7.9 267.0 %all-gather.28.cloned.1.call-start = ((), (), s32[]{:S(2)}) async-start(), calls=%async_computation.17 | async-start | bytes 5242880 | tf_op jit(solution)/shard_map/all_gather | solution.py:89
  156.9 124.7 %all-gather.26.cloned.1.call-start = ((), (), s32[]{:S(2)}) async-start(), calls=%async_computation.16 | async-start | bytes 5242880 | tf_op jit(solution)/shard_map/all_gather | solution.py:90
  198.4 139.2 %all-gather.20.cloned.1.call-start = ((), (), s32[]{:S(2)}) async-start(), calls=%async_computation.7 | async-start | bytes 8912896 | tf_op jit(solution)/shard_map/all_gather | solution.py:74
  199.0 277.4 %all-gather.22.cloned.1.call-start = ((), (), s32[]{:S(2)}) async-start(), calls=%async_computation.8 | async-start | bytes 35651584 | tf_op jit(solution)/shard_map/all_gather | solution.py:116
  199.6 446.3 %all-gather.24.cloned.1.call-start = ((), (), s32[]{:S(2)}) async-start(), calls=%async_computation.9 | async-start | bytes 35651584 | tf_op jit(solution)/shard_map/all_gather | solution.py:138
  200.1 676.9 %reduce-scatter.7.cloned.1.call-start = ((), (), s32[]{:S(2)}) async-start(), calls=%async_computation.10 | async-start | bytes 5242880 | tf_op jit(solution)/shard_map/reduce_scatter | solution.py:199
  343.9 562.8 %copy-start.10 = (f32[256,2048]{1,0:T(8,128)}, f32[256,2048]{1,0:T(8,128)S(1)}, u32[]{:S(2)}) copy-start(f32[256,2048]{1,0:T(8,128)S(1)} %get-tuple-element.55) | copy-start | bytes 6291460
  788.1 92.6 %reduce-scatter.9.cloned.1.call-start = ((), (), s32[]{:S(2)}) async-start(), calls=%async_computation.11 | async-start | bytes 5242880 | tf_op jit(solution)/shard_map/reduce_scatter | solution.py:205
  805.6 1685.6 %reduce-scatter.13.cloned.1.call-start = ((), (), s32[]{:S(2)}) async-start(), calls=%async_computation.13 | async-start | bytes 17825792 | tf_op jit(solution)/shard_map/reduce_scatter | solution.py:227
  815.7 1677.5 %reduce-scatter.11.cloned.1.call-start = ((), (), s32[]{:S(2)}) async-start(), calls=%async_computation.12 | async-start | bytes 53477376 | tf_op jit(solution)/shard_map/reduce_scatter | solution.py:224
  906.7 1976.1 %reduce-scatter.15.cloned.1.call-start = ((), (), s32[]{:S(2)}) async-start(), calls=%async_computation.14 | async-start | bytes 71303168 | tf_op jit(solution)/shard_map/reduce_scatter | solution.py:160
  934.5 2588.7 %reduce-scatter.17.cloned.1.call-start = ((), (), s32[]{:S(2)}) async-start(), calls=%async_computation.15 | async-start | bytes 71303168 | tf_op jit(solution)/shard_map/reduce_scatter | solution.py:162
  970.1 2710.5 %all-reduce.14.cloned.1.call-start = ((), (), s32[]{:S(2)}) async-start(), calls=%async_computation.18 | async-start | bytes 12582912 | tf_op jit(solution)/shard_map/psum | solution.py:233
  971.6 40.4 %collective-permute-start = (bf16[512,2048]{1,0:T(8,128)(2,1)S(1)}, bf16[512,2048]{1,0:T(8,128)(2,1)S(1)}, u32[]{:S(2)}, u32[]{:S(2)}) collective-permute-start(bf16[512,2048]{1,0:T(8,128)(2,1)S(1)} %copy-done.1), channel_id=1, source_target_pairs={{0,15},{1,0},{2,1},{3,2},{4,3},{5,4},{6,5},{7,6},{8,7},{9,8},{10,9... | collective-permute-start | bytes 6291464 | tf_op jit(solution)/shard_map/ppermute | solution.py:15
  1012.0 382.5 %copy-start.5 = (bf16[512,2048]{1,0:T(8,128)(2,1)}, bf16[512,2048]{1,0:T(8,128)(2,1)S(1)}, u32[]{:S(2)}) copy-start(bf16[512,2048]{1,0:T(8,128)(2,1)S(1)} %collective-permute-done) | copy-start | bytes 6291460
  1012.5 93.5 %collective-permute-start.1 = (bf16[1024,2048]{1,0:T(8,128)(2,1)S(1)}, bf16[1024,2048]{1,0:T(8,128)(2,1)S(1)}, u32[]{:S(2)}, u32[]{:S(2)}) collective-permute-start(bf16[1024,2048]{1,0:T(8,128)(2,1)S(1)} %pad_maximum_fusion.2), channel_id=1, source_target_pairs={{0,14},{1,15},{2,0},{3,1},{4,2},{5,3},{6,4},{7,5},{8,6},{9,7},{10,... | collective-permute-start | bytes 12582920 | tf_op jit(solution)/shard_map/ppermute | solution.py:15
  1106.0 288.4 %copy-start.2 = (bf16[1024,2048]{1,0:T(8,128)(2,1)}, bf16[1024,2048]{1,0:T(8,128)(2,1)S(1)}, u32[]{:S(2)}) copy-start(bf16[1024,2048]{1,0:T(8,128)(2,1)S(1)} %collective-permute-done.1) | copy-start | bytes 12582916
  1107.3 296.1 %copy-start.55 = (u32[32]{0:T(128)S(1)}, u32[32]{0:T(128)}, u32[]{:S(2)}) copy-start(u32[32]{0:T(128)} %constant.131) | copy-start | bytes 388
  1107.3 298.0 %copy-start.54 = (bf16[128]{0:T(256)(128)(2,1)S(1)}, bf16[128]{0:T(256)(128)(2,1)}, u32[]{:S(2)}) copy-start(bf16[128]{0:T(256)(128)(2,1)} %param.26) | copy-start | bytes 772
  1107.3 287.1 %collective-permute-start.2 = (bf16[2048,2048]{1,0:T(8,128)(2,1)S(1)}, bf16[2048,2048]{1,0:T(8,128)(2,1)S(1)}, u32[]{:S(2)}, u32[]{:S(2)}) collective-permute-start(bf16[2048,2048]{1,0:T(8,128)(2,1)S(1)} %pad_maximum_fusion.1), channel_id=1, source_target_pairs={{0,12},{1,13},{2,14},{3,15},{4,0},{5,1},{6,2},{7,3},{8,4},{9,5},{1... | collective-permute-start | bytes 25165832 | tf_op jit(solution)/shard_map/ppermute | solution.py:15
  1403.4 1044.6 %collective-permute-start.3 = (bf16[4096,2048]{1,0:T(8,128)(2,1)}, bf16[4096,2048]{1,0:T(8,128)(2,1)}, u32[]{:S(2)}, u32[]{:S(2)}) collective-permute-start(bf16[4096,2048]{1,0:T(8,128)(2,1)} %pad_maximum_fusion), channel_id=1, source_target_pairs={{0,8},{1,9},{2,10},{3,11},{4,12},{5,13},{6,14},{7,15},{8,0},{9,1},... | collective-permute-start | bytes 50331656 | tf_op jit(solution)/shard_map/ppermute | solution.py:15
  1824.6 639.2 %copy-start.6 = (bf16[512,2048]{1,0:T(8,128)(2,1)S(1)}, bf16[512,2048]{1,0:T(8,128)(2,1)}, u32[]{:S(2)}) copy-start(bf16[512,2048]{1,0:T(8,128)(2,1)} %copy-done.5) | copy-start | bytes 6291460
  2496.5 1030.5 %copy-start.11 = (f32[256,2048]{1,0:T(8,128)S(1)}, f32[256,2048]{1,0:T(8,128)}, u32[]{:S(2)}) copy-start(f32[256,2048]{1,0:T(8,128)} %copy-done.10) | copy-start | bytes 6291460
  (49 other events, 1890.0 us)
Sparse Core Ops, SparseCore 0:
  9.6 131.3 all-gather.17
  157.1 34.6 all-gather.27
  198.5 32.9 all-gather.25
  233.5 74.9 all-gather.19
  310.0 166.3 all-gather.21
  477.8 168.0 all-gather.23
  788.2 44.5 reduce-scatter.6
  836.0 44.5 reduce-scatter.8
  884.8 319.9 reduce-scatter.12
  1208.8 984.5 reduce-scatter.10
  2197.7 685.1 reduce-scatter.14
  2886.9 636.1 reduce-scatter.16
  3527.1 153.4 all-reduce.13
